TPU v7x, 1024 devices: a whole 8x8x8 slice. The times are simulated.
1024 devices in a mesh: energy: 64 (over y, x), slab: 16 (over z, core).
Axes of the slice: x: 8, y: 8, z: 8, core: 2. Of those that a mesh axis runs over, the one named last changes fastest.
Arguments:
- green_local: bfloat16 [64, 6144, 768], P('energy', 'slab'), may hold values from -6 to 6
- coupling: bfloat16 [6144, 384], P('slab'), may hold values from -0.3125 to 0.3125
- phonon_coupling: bfloat16 [3, 384, 384], replicated, may hold values from -0.3125 to 0.3125
- offsets: int32 [3], replicated, may hold values from 1 to 4, as said below
- bose_factors: float32 [3], replicated, may hold values from 0.2 to 3
Outputs:
- phonon_sigma: bfloat16 [64, 6144, 768], P('energy', 'slab')
- cumulative: float32 [64, 6144], P('energy', 'slab')
Inputs may be any that keep to these rules, and one draw needn't show every extreme that they name: The offsets are distinct, and one of them equals 4.
All inputs are finite; a program needn't handle non-finite values.
Results may differ from a plain program's by a relative error of at most 0.018.
Values may be sent and summed in bfloat16 or wider, within the bound.
A program may use at most 32 MiB of HBM per device.

v0:
```python
import jax
import jax.numpy as jnp
from jax import lax
from jax.sharding import PartitionSpec as P

M = 384
MODES = 3
OMAX = 4


def padded_2(shard, sides, width):
    for axis, dim in sides:
        devices, length = (lax.axis_size(axis), shard.shape[dim])
        up = [(i, (i + 1) % devices) for i in range(devices - 1)]
        down = [(j, i) for i, j in up]
        last = lax.slice_in_dim(shard, length - width, length, axis=dim)
        leading = lax.slice_in_dim(shard, 0, width, axis=dim)
        before = lax.ppermute(last, axis, up)
        after = lax.ppermute(leading, axis, down)
        shard = jnp.concatenate([before, shard, after], axis=dim)
    return shard


def from_behind(value, axis, steps):
    count = lax.axis_size(axis)
    leading, last = (max(0, -steps), min(count, count - steps))
    return lax.ppermute(value, axis, [(source, source + steps) for source in range(leading, last)])


def entering(part, axis, combine, identity):
    place = lax.axis_index(axis)
    gathered = lax.all_gather(part, axis)
    state = jnp.zeros_like(part) + jnp.asarray(identity, part.dtype)

    def one(hop, state):
        return combine(state, lax.dynamic_index_in_dim(gathered, hop, 0, False))

    return lax.fori_loop(0, place, one, state)


def left_real(matrices, blocks):
    return jnp.einsum("eab,ebc->eac", matrices, blocks, preferred_element_type=jnp.float32)


def right_real(blocks, matrices):
    batch_size, row_count, double = blocks.shape
    halves = blocks.reshape(batch_size, row_count, 2, double // 2)
    product = jnp.einsum("eatm,emb->eatb", halves, matrices, preferred_element_type=jnp.float32)
    return product.reshape(batch_size, row_count, double)


def complex_matrix(blocks):
    half_width = blocks.shape[-1] // 2
    real_part = blocks[..., :half_width]
    imag_part = blocks[..., half_width:]
    top_rows = jnp.concatenate([real_part, imag_part], axis=-1)
    bottom_rows = jnp.concatenate([-imag_part, real_part], axis=-1)
    return jnp.concatenate([top_rows, bottom_rows], axis=-2)


def complex_product(first, second):
    return jnp.einsum(
        "eam,emn->ean", first, complex_matrix(second), preferred_element_type=jnp.float32
    )


def add_vectors(earlier, later):
    return earlier + later


def body(green_local, coupling, phonon_coupling, offsets, bose_factors):
    local_count, row_count, double = green_local.shape
    links = coupling[None]
    links_transposed = jnp.swapaxes(links, 1, 2)
    padded = padded_2(green_local, (("slab", 1),), row_count)
    lower_blocks = padded[:, :row_count]
    upper_blocks = padded[:, 2 * row_count :]
    lower_link = from_behind(coupling, "slab", 1)
    lower_links = lower_link[None]
    down_left = left_real(jnp.swapaxes(lower_links, 1, 2), lower_blocks).astype(jnp.bfloat16)
    lower_term = right_real(down_left, lower_links).astype(jnp.bfloat16)
    up_left = left_real(links, upper_blocks).astype(jnp.bfloat16)
    upper_term = right_real(up_left, links_transposed).astype(jnp.bfloat16)
    couple = (upper_term.astype(jnp.float32) + lower_term.astype(jnp.float32)).astype(jnp.bfloat16)
    dressed = complex_product(green_local, couple).astype(jnp.bfloat16)
    greens = (green_local.astype(jnp.float32) + complex_product(dressed, green_local) / M).astype(
        jnp.bfloat16
    )
    hop_count = (OMAX + local_count - 1) // local_count
    lower_list = [from_behind(greens, "energy", distance) for distance in range(hop_count, 0, -1)]
    upper_list = [from_behind(greens, "energy", -distance) for distance in range(1, hop_count + 1)]
    window_low = jnp.concatenate(lower_list + [greens], axis=0)
    window_high = jnp.concatenate([greens] + upper_list, axis=0)
    accumulated = jnp.zeros((local_count, row_count, double), jnp.float32)
    for mode_index in range(MODES):
        shift_size = offsets[mode_index]
        lower_block = lax.dynamic_slice_in_dim(
            window_low, hop_count * local_count - shift_size, local_count, 0
        )
        upper_block = lax.dynamic_slice_in_dim(window_high, shift_size, local_count, 0)
        factor = bose_factors[mode_index]
        mixture = (
            (factor + 1.0) * lower_block.astype(jnp.float32)
            + factor * upper_block.astype(jnp.float32)
        ).astype(jnp.bfloat16)
        matrices = phonon_coupling[mode_index][None]
        phonon_left = left_real(matrices, mixture).astype(jnp.bfloat16)
        accumulated = accumulated + right_real(phonon_left, jnp.swapaxes(matrices, 1, 2))
    phonon_sigma = accumulated.astype(jnp.bfloat16)
    energies = local_count * lax.axis_size("energy")
    positions = (
        lax.axis_index("energy") * local_count + jnp.arange(local_count, dtype=jnp.int32)
    ).astype(jnp.float32)
    holes = jax.nn.sigmoid((positions + 0.5 - energies / 2) * 4.0 / energies)
    imag_diag = jnp.diagonal(greens[..., row_count:], axis1=1, axis2=2).astype(jnp.float32)
    dos_terms = -holes[:, None] * imag_diag
    block_total = jnp.sum(dos_terms, axis=0)
    prefix = entering(block_total, "energy", add_vectors, jnp.zeros((row_count,), jnp.float32))
    cumulative = prefix[None] + jnp.cumsum(dos_terms, axis=0)
    return (phonon_sigma, cumulative)


def solution(mesh):
    in_specs = (P("energy", "slab", None), P("slab", None), P(), P(), P())
    out_specs = (P("energy", "slab", None), P("energy", "slab"))
    return jax.shard_map(body, mesh=mesh, in_specs=in_specs, out_specs=out_specs, check_vma=False)
```

profile of v0, /device:TPU:442, one launch (start us, length us, event | category | flops | bytes accessed | tf_op | source)
XLA Modules:
  0.0 278.7 jit_solution(5534537310575221680)
XLA Ops:
  0.6 2.1 collective-permute-start
  2.7 2.4 collective-permute-start.2
  5.1 1.2 copy.22
  6.3 6.0 %collective-permute-start.1 = (bf16[384,384]{0,1:T(8,128)(2,1)S(1)}, bf16[384,384]{0,1:T(8,128)(2,1)S(1)}, u32[]{:S(2)}, u32[]{:S(2)}) collective-permute-start(bf16[384,384]{0,1:T(8,128)(2,1)S(1)} %copy.22), channel_id=1, source_target_pairs={{0,1},{1,2},{2,3},{3,4},{4,5},{5,6},{6,7},{7,8},{8,9},{9,10},{10,1... | collective-permute-start | bytes 884744 | tf_op jit(solution)/shard_map/ppermute | solution.py:27
  12.3 1.4 fusion.64
  13.7 1.1 slice_negate_fusion.1
  14.9 0.6 fusion.63
  27.5 0.5 fusion.7
  28.4 0.5 fusion.6
  29.0 1.0 copy-done.2
  30.0 1.6 fusion.2
  31.6 5.6 %collective-permute-start.3 = (bf16[1,384,768]{2,1,0:T(8,128)(2,1)S(1)}, bf16[1,384,768]{2,1,0:T(8,128)(2,1)}, u32[]{:S(2)}, u32[]{:S(2)}) collective-permute-start(bf16[1,384,768]{2,1,0:T(8,128)(2,1)S(1)} %fusion.2), channel_id=1, source_target_pairs={{0,64},{16,80},{32,96},{48,112},{64,128},{80,144},{96,160},{112,17... | collective-permute-start | bytes 1769480 | tf_op jit(solution)/shard_map/ppermute | solution.py:27
  37.2 6.5 %collective-permute-start.4 = (bf16[1,384,768]{2,1,0:T(8,128)(2,1)S(1)}, bf16[1,384,768]{2,1,0:T(8,128)(2,1)S(1)}, u32[]{:S(2)}, u32[]{:S(2)}) collective-permute-start(bf16[1,384,768]{2,1,0:T(8,128)(2,1)S(1)} %fusion.2), channel_id=1, source_target_pairs={{0,48},{16,64},{32,80},{48,96},{64,112},{80,128},{96,144},{112,160... | collective-permute-start | bytes 1769480 | tf_op jit(solution)/shard_map/ppermute | solution.py:27
  43.7 2.5 collective-permute-start.5
  46.2 2.5 collective-permute-start.6
  48.7 3.3 %collective-permute-start.7 = (bf16[1,384,768]{2,1,0:T(8,128)(2,1)S(1)}, bf16[1,384,768]{2,1,0:T(8,128)(2,1)S(1)}, u32[]{:S(2)}, u32[]{:S(2)}) collective-permute-start(bf16[1,384,768]{2,1,0:T(8,128)(2,1)S(1)} %fusion.2), channel_id=1, source_target_pairs={{16,0},{32,16},{48,32},{64,48},{80,64},{96,80},{112,96},{128,112},... | collective-permute-start | bytes 1769480 | tf_op jit(solution)/shard_map/ppermute | solution.py:27
  52.1 3.7 %gather_fusion = bf16[384]{0:T(512)(128)(2,1)S(1)} fusion(bf16[384,384]{1,0:T(8,128)(2,1)S(1)} %slice_bitcast_fusion, s32[384]{0:T(512)S(1)} %or_reduce_fusion), kind=kCustom, calls=%fused_computation | custom fusion | bytes 4608 | tf_op jit(solution)/shard_map/jit(diagonal)/gather | solution.py:115
  55.8 129.2 %all-gather.1 = f32[64,1,384]{2,1,0:T(1,128)S(1)} all-gather(f32[1,1,384]{2,1,0:T(1,128)S(1)} %reshape.260), channel_id=2, replica_groups=mesh['energy'=64,'slab'=16] {'energy'}, dimensions={0}, use_global_device_ids=true | all-gather | bytes 99840 | tf_op jit(solution)/shard_map/all_gather | solution.py:32
  185.0 1.8 while.10
  186.8 0.6 add.127
  187.4 1.9 collective-permute-start.8
  189.3 1.1 constant_dynamic-update-slice_fusion.4
  190.4 3.2 %collective-permute-start.9 = (bf16[1,384,768]{2,1,0:T(8,128)(2,1)S(1)}, bf16[1,384,768]{2,1,0:T(8,128)(2,1)S(1)}, u32[]{:S(2)}, u32[]{:S(2)}) collective-permute-start(bf16[1,384,768]{2,1,0:T(8,128)(2,1)S(1)} %fusion.2), channel_id=1, source_target_pairs={{48,0},{64,16},{80,32},{96,48},{112,64},{128,80},{144,96},{160,112... | collective-permute-start | bytes 1769480 | tf_op jit(solution)/shard_map/ppermute | solution.py:27
  193.7 4.2 %collective-permute-start.10 = (bf16[1,384,768]{2,1,0:T(8,128)(2,1)S(1)}, bf16[1,384,768]{2,1,0:T(8,128)(2,1)S(1)}, u32[]{:S(2)}, u32[]{:S(2)}) collective-permute-start(bf16[1,384,768]{2,1,0:T(8,128)(2,1)S(1)} %fusion.2), channel_id=1, source_target_pairs={{64,0},{80,16},{96,32},{112,48},{128,64},{144,80},{160,96},{176,11... | collective-permute-start | bytes 1769480 | tf_op jit(solution)/shard_map/ppermute | solution.py:27
  198.1 26.7 %collective-permute-done.8 = bf16[1,384,768]{2,1,0:T(8,128)(2,1)S(1)} collective-permute-done((bf16[1,384,768]{2,1,0:T(8,128)(2,1)S(1)}, bf16[1,384,768]{2,1,0:T(8,128)(2,1)S(1)}, u32[]{:S(2)}, u32[]{:S(2)}) %collective-permute-start.8) | collective-permute-done | bytes 589856 | tf_op jit(solution)/shard_map/ppermute | solution.py:27
  224.8 29.8 %collective-permute-done.9 = bf16[1,384,768]{2,1,0:T(8,128)(2,1)S(1)} collective-permute-done((bf16[1,384,768]{2,1,0:T(8,128)(2,1)S(1)}, bf16[1,384,768]{2,1,0:T(8,128)(2,1)S(1)}, u32[]{:S(2)}, u32[]{:S(2)}) %collective-permute-start.9) | collective-permute-done | bytes 589856 | tf_op jit(solution)/shard_map/ppermute | solution.py:27
  254.7 17.9 %collective-permute-done.10 = bf16[1,384,768]{2,1,0:T(8,128)(2,1)S(1)} collective-permute-done((bf16[1,384,768]{2,1,0:T(8,128)(2,1)S(1)}, bf16[1,384,768]{2,1,0:T(8,128)(2,1)S(1)}, u32[]{:S(2)}, u32[]{:S(2)}) %collective-permute-start.10) | collective-permute-done | bytes 589856 | tf_op jit(solution)/shard_map/ppermute | solution.py:27
  272.7 1.2 convolution_convert_fusion.2
  274.3 1.1 convolution_convert_fusion.1
  275.9 1.2 convolution_convert_fusion
  277.1 0.5 fusion.3
  277.6 1.1 copy.27
  (93 shorter events, 3.5 us)
Async XLA Ops:
  0.6 26.3 %copy-start = (bf16[384,384]{1,0:T(8,128)(2,1)S(1)}, bf16[384,384]{1,0:T(8,128)(2,1)}, u32[]{:S(2)}) copy-start(bf16[384,384]{1,0:T(8,128)(2,1)} %param.8) | copy-start | bytes 884740
  0.6 14.2 %copy-start.3 = (f32[3]{0:T(128)S(1)}, f32[3]{0:T(128)}, u32[]{:S(2)}) copy-start(f32[3]{0:T(128)} %param.11) | copy-start | bytes 40
  0.6 26.3 %collective-permute-start = (bf16[1,384,768]{2,1,0:T(8,128)(2,1)}, bf16[1,384,768]{2,1,0:T(8,128)(2,1)S(1)}, u32[]{:S(2)}, u32[]{:S(2)}) collective-permute-start(bf16[1,384,768]{2,1,0:T(8,128)(2,1)} %param.7), channel_id=1, source_target_pairs={{1,0},{2,1},{3,2},{4,3},{5,4},{6,5},{7,6},{8,7},{9,8},{10,9},{11,1... | collective-permute-start | bytes 1769480 | tf_op jit(solution)/shard_map/ppermute | solution.py:19
  2.7 25.2 %collective-permute-start.2 = (bf16[1,384,768]{2,1,0:T(8,128)(2,1)}, bf16[1,384,768]{2,1,0:T(8,128)(2,1)S(1)}, u32[]{:S(2)}, u32[]{:S(2)}) collective-permute-start(bf16[1,384,768]{2,1,0:T(8,128)(2,1)} %param.7), channel_id=1, source_target_pairs={{0,1},{1,2},{2,3},{3,4},{4,5},{5,6},{6,7},{7,8},{8,9},{9,10},{10,1... | collective-permute-start | bytes 1769480 | tf_op jit(solution)/shard_map/ppermute | solution.py:18
  6.3 21.6 %collective-permute-start.1 = (bf16[384,384]{0,1:T(8,128)(2,1)S(1)}, bf16[384,384]{0,1:T(8,128)(2,1)S(1)}, u32[]{:S(2)}, u32[]{:S(2)}) collective-permute-start(bf16[384,384]{0,1:T(8,128)(2,1)S(1)} %copy.22), channel_id=1, source_target_pairs={{0,1},{1,2},{2,3},{3,4},{4,5},{5,6},{6,7},{7,8},{8,9},{9,10},{10,1... | collective-permute-start | bytes 884744 | tf_op jit(solution)/shard_map/ppermute | solution.py:27
  28.9 1.1 copy-start.2
  31.6 155.8 %collective-permute-start.3 = (bf16[1,384,768]{2,1,0:T(8,128)(2,1)S(1)}, bf16[1,384,768]{2,1,0:T(8,128)(2,1)}, u32[]{:S(2)}, u32[]{:S(2)}) collective-permute-start(bf16[1,384,768]{2,1,0:T(8,128)(2,1)S(1)} %fusion.2), channel_id=1, source_target_pairs={{0,64},{16,80},{32,96},{48,112},{64,128},{80,144},{96,160},{112,17... | collective-permute-start | bytes 1769480 | tf_op jit(solution)/shard_map/ppermute | solution.py:27
  37.2 153.2 %collective-permute-start.4 = (bf16[1,384,768]{2,1,0:T(8,128)(2,1)S(1)}, bf16[1,384,768]{2,1,0:T(8,128)(2,1)S(1)}, u32[]{:S(2)}, u32[]{:S(2)}) collective-permute-start(bf16[1,384,768]{2,1,0:T(8,128)(2,1)S(1)} %fusion.2), channel_id=1, source_target_pairs={{0,48},{16,64},{32,80},{48,96},{64,112},{80,128},{96,144},{112,160... | collective-permute-start | bytes 1769480 | tf_op jit(solution)/shard_map/ppermute | solution.py:27
  43.7 150.0 %collective-permute-start.5 = (bf16[1,384,768]{2,1,0:T(8,128)(2,1)S(1)}, bf16[1,384,768]{2,1,0:T(8,128)(2,1)S(1)}, u32[]{:S(2)}, u32[]{:S(2)}) collective-permute-start(bf16[1,384,768]{2,1,0:T(8,128)(2,1)S(1)} %fusion.2), channel_id=1, source_target_pairs={{0,32},{16,48},{32,64},{48,80},{64,96},{80,112},{96,128},{112,144}... | collective-permute-start | bytes 1769480 | tf_op jit(solution)/shard_map/ppermute | solution.py:27
  46.2 151.7 %collective-permute-start.6 = (bf16[1,384,768]{2,1,0:T(8,128)(2,1)S(1)}, bf16[1,384,768]{2,1,0:T(8,128)(2,1)S(1)}, u32[]{:S(2)}, u32[]{:S(2)}) collective-permute-start(bf16[1,384,768]{2,1,0:T(8,128)(2,1)S(1)} %fusion.2), channel_id=1, source_target_pairs={{0,16},{16,32},{32,48},{48,64},{64,80},{80,96},{96,112},{112,128},... | collective-permute-start | bytes 1769480 | tf_op jit(solution)/shard_map/ppermute | solution.py:27
  48.7 149.3 %collective-permute-start.7 = (bf16[1,384,768]{2,1,0:T(8,128)(2,1)S(1)}, bf16[1,384,768]{2,1,0:T(8,128)(2,1)S(1)}, u32[]{:S(2)}, u32[]{:S(2)}) collective-permute-start(bf16[1,384,768]{2,1,0:T(8,128)(2,1)S(1)} %fusion.2), channel_id=1, source_target_pairs={{16,0},{32,16},{48,32},{64,48},{80,64},{96,80},{112,96},{128,112},... | collective-permute-start | bytes 1769480 | tf_op jit(solution)/shard_map/ppermute | solution.py:27
  187.4 37.4 %collective-permute-start.8 = (bf16[1,384,768]{2,1,0:T(8,128)(2,1)S(1)}, bf16[1,384,768]{2,1,0:T(8,128)(2,1)S(1)}, u32[]{:S(2)}, u32[]{:S(2)}) collective-permute-start(bf16[1,384,768]{2,1,0:T(8,128)(2,1)S(1)} %fusion.2), channel_id=1, source_target_pairs={{32,0},{48,16},{64,32},{80,48},{96,64},{112,80},{128,96},{144,112}... | collective-permute-start | bytes 1769480 | tf_op jit(solution)/shard_map/ppermute | solution.py:27
  190.4 64.2 %collective-permute-start.9 = (bf16[1,384,768]{2,1,0:T(8,128)(2,1)S(1)}, bf16[1,384,768]{2,1,0:T(8,128)(2,1)S(1)}, u32[]{:S(2)}, u32[]{:S(2)}) collective-permute-start(bf16[1,384,768]{2,1,0:T(8,128)(2,1)S(1)} %fusion.2), channel_id=1, source_target_pairs={{48,0},{64,16},{80,32},{96,48},{112,64},{128,80},{144,96},{160,112... | collective-permute-start | bytes 1769480 | tf_op jit(solution)/shard_map/ppermute | solution.py:27
  193.7 78.9 %collective-permute-start.10 = (bf16[1,384,768]{2,1,0:T(8,128)(2,1)S(1)}, bf16[1,384,768]{2,1,0:T(8,128)(2,1)S(1)}, u32[]{:S(2)}, u32[]{:S(2)}) collective-permute-start(bf16[1,384,768]{2,1,0:T(8,128)(2,1)S(1)} %fusion.2), channel_id=1, source_target_pairs={{64,0},{80,16},{96,32},{112,48},{128,64},{144,80},{160,96},{176,11... | collective-permute-start | bytes 1769480 | tf_op jit(solution)/shard_map/ppermute | solution.py:27
  224.8 47.8 %copy-start.1 = (bf16[3,384,384]{2,1,0:T(8,128)(2,1)S(1)}, bf16[3,384,384]{2,1,0:T(8,128)(2,1)}, u32[]{:S(2)}) copy-start(bf16[3,384,384]{2,1,0:T(8,128)(2,1)} %param.9) | copy-start | bytes 2654212
where the time goes:
time: 279 us
  blocking collectives  129 us (46%)
  waiting for transfers between devices  74.4 us (27%)
  starting transfers between devices  40.2 us (14%)
  between operations  12.5 us (4%)
  local copies, waits for them, and re-layouts  11.8 us (4%)
  matrix products  8.43 us (3%)
    all_gather x1, blocking collectives, entering(): gathered = lax.all_gather(part, axis)  129 us
    ppermute x9, waiting for transfers between devices, from_behind(): lax.ppermute(value, axis, [(source, source + steps) for source in range(l...  74.4 us
    ppermute x9, starting transfers between devices, from_behind(): lax.ppermute(value, axis, [(source, source + steps) for source in range(l...  35.7 us
  transfers between devices with their start and end apart: 11, of which 3 were waited for; matrix products, arithmetic and copies ran while one was open for 4% of the time, Pallas kernels for 0%

commit v1 on v0

v1 whole, which is shorter than its diff:
```python
import functools

import jax
import jax.numpy as jnp
from jax import lax
from jax.experimental import pallas as pl
from jax.experimental.pallas import tpu as pltpu
from jax.sharding import PartitionSpec as P

M = 384
MODES = 3
ROW = 8
CHUNKS = 2
ROWS = M // CHUNKS
MESH = pl.DeviceIdType.MESH
F32 = jnp.float32
BF16 = jnp.bfloat16

ROUTES = {
    (1, 2, 3, 4): {
        "right": [(0, 0, 1), (0, 1, 2), (0, 2, 3), (0, 3, 4), (1, 0, 1), (1, 1, 2), (1, 2, 3)],
        "down": [(0, 4, -4)],
    },
}


def slot_of(offset):
    return offset + 4 if offset < 0 else offset + 3


def plan(distances, chunk_us=3.2, latency_us=1.6):
    base = ROUTES[distances]
    links = {
        "right": base["right"],
        "left": [(1 - h, -a, -b) for h, a, b in base["right"]],
        "down": base["down"],
        "up": [(1 - h, -a, -b) for h, a, b in base["down"]],
    }
    ready = {(h, 0, c): 0.8 * c for h in range(2) for c in range(CHUNKS)}
    queues = {name: [(h, a, b, c) for h, a, b in routes for c in range(CHUNKS)] for name, routes in links.items()}
    free = {name: 0.0 for name in links}
    last = {name: 0.0 for name in links}
    events = []
    while any(queues.values()):
        for name, queue in queues.items():
            while queue and (queue[0][0], queue[0][1], queue[0][3]) in ready:
                h, a, b, c = queue.pop(0)
                source = ready[(h, a, c)]
                last[name] = max(last[name], source)
                free[name] = max(free[name], source) + chunk_us
                ready[(h, b, c)] = free[name] + latency_us
                events.append((last[name], 0, ("send", h, a, b, c)))
    for d in distances:
        for h in range(2):
            when = max(ready[(h, o, c)] for o in (-d, d) for c in range(CHUNKS))
            events.append((when, 1, ("product", d, h)))
    after = max(ready[(0, 1, c)] for c in range(CHUNKS))
    for order, name in enumerate(("sum4", "sum8", "sum32", "sum64")):
        events.append((after + 6.4 * order, 2, (name,)))
    events.sort(key=lambda event: event[:2])
    return [event[2] for event in events]


def mm(a, b):
    return jnp.dot(a, b, preferred_element_type=F32)


def kernel(
    distances, energies, slabs,
    g_hbm, b_hbm, p_hbm, off_ref, bose_ref,
    sigma_ref, cum_ref,
    gv, bv, bt, pv, pt, gup, low_in, low_out, couple, greens, slots, acc,
    own_sum, own4, own8, own32, got1, got4, got8, got32,
    load_sem, zsend, zrecv, hsend, hrecv, ssend, srecv, tokens,
):
    e = lax.axis_index("energy")
    s = lax.axis_index("slab")
    first = s == 0
    last = s == slabs - 1

    def at(step):
        return lax.rem(e + (step + energies), energies)

    near = (1, -1, ROW, -ROW)
    barrier = pltpu.get_barrier_semaphore()
    for step in near:
        pl.semaphore_signal(barrier, inc=1, device_id=(at(step), s), device_id_type=MESH)

    @pl.when(s > 0)
    def _():
        pl.semaphore_signal(barrier, inc=1, device_id=(e, s - 1), device_id_type=MESH)

    @pl.when(s < slabs - 1)
    def _():
        pl.semaphore_signal(barrier, inc=1, device_id=(e, s + 1), device_id_type=MESH)

    loads = [
        pltpu.make_async_copy(g_hbm.at[0, :, pl.ds(0, M)], gv.at[0], load_sem.at[0]),
        pltpu.make_async_copy(b_hbm, bv, load_sem.at[1]),
        pltpu.make_async_copy(g_hbm.at[0, :, pl.ds(M, M)], gv.at[1], load_sem.at[2]),
        pltpu.make_async_copy(p_hbm, pv, load_sem.at[3]),
    ]
    for load in loads:
        load.start()

    slab_links = jnp.where(first, 0, 1) + jnp.where(last, 0, 1)
    pl.semaphore_wait(barrier, len(near) + slab_links)

    downs = [
        pltpu.make_async_remote_copy(
            src_ref=g_hbm.at[0, :, pl.ds(h * M, M)], dst_ref=gup.at[h],
            send_sem=zsend.at[h], recv_sem=zrecv.at[h],
            device_id=(e, s - 1), device_id_type=MESH)
        for h in range(2)
    ]
    ups = [
        pltpu.make_async_remote_copy(
            src_ref=low_out.at[h], dst_ref=low_in.at[h],
            send_sem=zsend.at[2 + h], recv_sem=zrecv.at[2 + h],
            device_id=(e, s + 1), device_id_type=MESH)
        for h in range(2)
    ]

    @pl.when(s > 0)
    def _():
        for copy in downs:
            copy.start()

    def token(index):
        for step in near:
            pl.semaphore_signal(tokens.at[index], inc=1, device_id=(at(step), s), device_id_type=MESH)

    token(0)

    loads[1].wait()
    bt[...] = bv[...].T
    for h in range(2):
        loads[0 if h == 0 else 2].wait()

        @pl.when(s < slabs - 1)
        def _():
            left = mm(bt[...], gv[h]).astype(BF16)
            low_out[h] = mm(left, bv[...]).astype(BF16)
            ups[h].start()

    pl.semaphore_wait(tokens.at[0], len(near))
    token(1)

    @pl.when(s < slabs - 1)
    def _():
        for h in range(2):
            downs[h].wait_recv()
            left = mm(bv[...], gup[h]).astype(BF16)
            couple[h] = mm(left, bt[...]).astype(BF16)

    @pl.when(last)
    def _():
        couple[...] = jnp.zeros_like(couple)

    pl.semaphore_wait(tokens.at[1], len(near))
    token(2)

    @pl.when(s > 0)
    def _():
        for h in range(2):
            ups[h].wait_recv()
            couple[h] = (couple[h].astype(F32) + low_in[h].astype(F32)).astype(BF16)

    pl.semaphore_wait(tokens.at[2], len(near))

    sends = {}

    def send(h, a, b, c):
        rows = pl.ds(c * ROWS, ROWS)
        source = greens.at[h, rows] if a == 0 else slots.at[slot_of(a), h, rows]
        index = len(sends)
        copy = pltpu.make_async_remote_copy(
            src_ref=source, dst_ref=slots.at[slot_of(b), h, rows],
            send_sem=hsend.at[index], recv_sem=hrecv.at[index],
            device_id=(at(b - a), s), device_id_type=MESH)
        copy.start()
        sends[(h, b, c)] = copy

    got = set()

    def arrived(h, o, c):
        if o != 0 and (h, o, c) not in got:
            got.add((h, o, c))
            sends[(h, o, c)].wait_recv()

    steps = plan(distances)
    early = [step for step in steps if step[0] == "send" and step[2] == 0]
    inv = 1.0 / M
    for c in range(CHUNKS):
        rows = pl.ds(c * ROWS, ROWS)
        gr, gi = gv[0, rows], gv[1, rows]
        dr = (mm(gr, couple[0]) - mm(gi, couple[1])).astype(BF16)
        di = (mm(gr, couple[1]) + mm(gi, couple[0])).astype(BF16)
        outr = mm(dr, gv[0]) - mm(di, gv[1])
        greens[0, rows] = (gr.astype(F32) + outr * inv).astype(BF16)
        outi = mm(dr, gv[1]) + mm(di, gv[0])
        greens[1, rows] = (gi.astype(F32) + outi * inv).astype(BF16)
        for step in early:
            if step[4] == c and (step[1], step[3]) in ((0, 1), (1, -1)):
                send(*step[1:])

    eye = lax.broadcasted_iota(jnp.int32, (128, 128), 0) == lax.broadcasted_iota(jnp.int32, (128, 128), 1)
    position = (e.astype(F32) + 0.5 - energies / 2) * 4.0 / energies
    holes = 1.0 / (1.0 + jnp.exp(-jnp.full((1, 128), position, F32)))
    for b in range(M // 128):
        block = greens[1, pl.ds(b * 128, 128), pl.ds(b * 128, 128)].astype(F32)
        diag = jnp.sum(jnp.where(eye, block, 0.0), axis=0, keepdims=True)
        own_sum[:, pl.ds(b * 128, 128)] = -holes * diag

    small = {}

    def small_send(name, index, source, target, step):
        copy = pltpu.make_async_remote_copy(
            src_ref=source, dst_ref=target, send_sem=ssend.at[index], recv_sem=srecv.at[index],
            device_id=(at(step), s), device_id_type=MESH)
        copy.start()
        small[(name, index)] = copy

    for j in range(3):
        small_send("one", j, own_sum, got1.at[j], j + 1)

    def take(name, base, count, stride, got_ref, value):
        for j in range(count):
            small[(name, base + j)].wait_recv()
            keep = jnp.where(e >= (j + 1) * stride, 1.0, 0.0)
            value = value + got_ref[j] * keep
        return value

    def sum4():
        own4[...] = take("one", 0, 3, 1, got1, own_sum[...])
        small_send("four", 3, own4, got4.at[0], 4)

    def sum8():
        own8[...] = take("four", 3, 1, 4, got4, own4[...])
        for j in range(3):
            small_send("eight", 4 + j, own8, got8.at[j], ROW * (j + 1))

    def sum32():
        own32[...] = take("eight", 4, 3, 8, got8, own8[...])
        small_send("rest", 7, own32, got32.at[0], 32)

    def sum64():
        cum_ref[...] = take("rest", 7, 1, 32, got32, own32[...])

    sums = {"sum4": sum4, "sum8": sum8, "sum32": sum32, "sum64": sum64}

    for k in range(MODES):
        if k == 0:
            loads[3].wait()
        pt[k] = pv[k].T

    started = []

    def product(d, h):
        for o in (d, -d):
            for c in range(CHUNKS):
                arrived(h, o, c)
        mode = jnp.int32(0)
        factor = F32(0.0)
        has = F32(0.0)
        for k in range(MODES):
            same = off_ref[k] == d
            mode = jnp.where(same, k, mode)
            factor = jnp.where(same, bose_ref[k], factor)
            has = jnp.where(same, 1.0, has)
        low = jnp.where(e >= d, (factor + 1.0) * has, 0.0)
        high = jnp.where(e < energies - d, factor * has, 0.0)
        mix = (low * slots[slot_of(d), h].astype(F32) + high * slots[slot_of(-d), h].astype(F32)).astype(BF16)
        left = mm(pv[mode], mix).astype(BF16)
        part = mm(left, pt[mode])
        if h in started:
            part = acc[h] + part
        started.append(h)
        if started.count(h) == len(distances):
            sigma_ref[0, :, pl.ds(h * M, M)] = part.astype(BF16)
        else:
            acc[h] = part

    for step in steps:
        if step[0] == "send":
            if (step[1], step[3], step[4]) in sends:
                continue
            arrived(step[1], step[2], step[4])
            send(*step[1:])
        elif step[0] == "product":
            product(*step[1:])
        else:
            sums[step[0]]()

    for copy in sends.values():
        copy.wait_send()
    for copy in small.values():
        copy.wait_send()

    @pl.when(s > 0)
    def _():
        for copy in downs:
            copy.wait_send()

    @pl.when(s < slabs - 1)
    def _():
        for copy in ups:
            copy.wait_send()


def body(green_local, coupling, phonon_coupling, offsets, bose_factors, distances):
    energies = lax.axis_size("energy")
    slabs = lax.axis_size("slab")
    any_spec = pl.BlockSpec(memory_space=pl.ANY)
    smem_spec = pl.BlockSpec(memory_space=pltpu.SMEM)
    vmem_spec = pl.BlockSpec(memory_space=pltpu.VMEM)
    hops = CHUNKS * 2 * sum(len(routes) for routes in ROUTES[distances].values())
    half = (M, M)
    return pl.pallas_call(
        functools.partial(kernel, distances, energies, slabs),
        out_shape=(
            jax.ShapeDtypeStruct((1, M, 2 * M), BF16),
            jax.ShapeDtypeStruct((1, M), F32),
        ),
        in_specs=[any_spec, any_spec, any_spec, smem_spec, smem_spec],
        out_specs=(vmem_spec, vmem_spec),
        scratch_shapes=[
            pltpu.VMEM((2, *half), BF16),
            pltpu.VMEM(half, BF16),
            pltpu.VMEM(half, BF16),
            pltpu.VMEM((MODES, *half), BF16),
            pltpu.VMEM((MODES, *half), BF16),
            pltpu.VMEM((2, *half), BF16),
            pltpu.VMEM((2, *half), BF16),
            pltpu.VMEM((2, *half), BF16),
            pltpu.VMEM((2, *half), BF16),
            pltpu.VMEM((2, *half), BF16),
            pltpu.VMEM((8, 2, *half), BF16),
            pltpu.VMEM((2, *half), F32),
            pltpu.VMEM((1, M), F32),
            pltpu.VMEM((1, M), F32),
            pltpu.VMEM((1, M), F32),
            pltpu.VMEM((1, M), F32),
            pltpu.VMEM((3, 1, M), F32),
            pltpu.VMEM((1, 1, M), F32),
            pltpu.VMEM((3, 1, M), F32),
            pltpu.VMEM((1, 1, M), F32),
            pltpu.SemaphoreType.DMA((4,)),
            pltpu.SemaphoreType.DMA((4,)),
            pltpu.SemaphoreType.DMA((4,)),
            pltpu.SemaphoreType.DMA((hops,)),
            pltpu.SemaphoreType.DMA((hops,)),
            pltpu.SemaphoreType.DMA((8,)),
            pltpu.SemaphoreType.DMA((8,)),
            pltpu.SemaphoreType.REGULAR((3,)),
        ],
        compiler_params=pltpu.CompilerParams(collective_id=0, has_side_effects=True),
    )(green_local, coupling, phonon_coupling, offsets, bose_factors)


def solution(mesh):
    in_specs = (P("energy", "slab", None), P("slab", None), P(), P(), P())
    out_specs = (P("energy", "slab", None), P("energy", "slab"))
    run = functools.partial(body, distances=(1, 2, 3, 4))
    return jax.shard_map(run, mesh=mesh, in_specs=in_specs, out_specs=out_specs, check_vma=False)
```

time: 279 us -> 87.2 us (0.31)
  the two profiles are of different devices: /device:TPU:442 before, /device:TPU:640 now
where the time goes in v1:
time: 87.2 us; the launch traced here: 87 us
  Pallas kernels  83.9 us (96%)
  local copies, waits for them, and re-layouts  2.48 us (3%)
    pallas_call x1, Pallas kernels, body(): pl.pallas_call(functools.partial(kernel, distances, energies, slabs), out...  83.9 us
    unnamed x4, local copies, waits for them, and re-layouts  2.48 us

profile of v1, /device:TPU:640, one launch (start us, length us, event | category | flops | bytes accessed | tf_op | source)
XLA Modules:
  0.0 87.0 jit_solution(2132586891560976344)
XLA Ops:
  0.6 83.9 %shard_map.68 = (bf16[1,384,768]{2,1,0:T(8,128)(2,1)}, f32[1,384]{1,0:T(1,128)}) custom-call(bf16[1,384,768]{2,1,0:T(8,128)(2,1)} %g_hbm.1, bf16[384,384]{1,0:T(8,128)(2,1)} %b_hbm.1, bf16[3,384,384]{2,1,0:T(8,128)(2,1)} %p_hbm.1, s32[3]{0:T(128)} %off_ref.1, f32[3]{0:T(128)} %bose_ref.1), custom_call_target="tpu_custom_call" | custom-call | tf_op jit(solution)/shard_map/pallas_call | solution.py:319
  84.5 0.0 copy-start
  84.5 1.9 %copy.9 = bf16[1,384,768]{2,1,0:T(8,128)(2,1)} copy(bf16[1,384,768]{2,1,0:T(8,128)(2,1)} %get-tuple-element.4) | data formatting | bytes 1179648
  86.5 0.0 copy-done
  86.5 0.6 copy.10
Async XLA Ops:
  84.5 1.9 %copy-start = (f32[1,384]{1,0:T(1,128)S(1)}, f32[1,384]{1,0:T(1,128)}, u32[]{:S(2)}) copy-start(f32[1,384]{1,0:T(1,128)} %get-tuple-element.5) | copy-start | bytes 4612
